TPU v7x, 256 devices: a whole 4x4x8 slice. The times are simulated.
256 devices in a mesh: space: 8 (over y, core), tm: 32 (over x, z).
Axes of the slice: x: 4, y: 4, z: 8, core: 2. Of those that a mesh axis runs over, the one named last changes fastest.
Arguments:
- snapshots: bfloat16 [8192, 32768], P('space', 'tm'), may hold values from -6 to 6
- basis: bfloat16 [8192, 64], P('space'), may hold values from -0.0625 to 0.0625
- lengths: int32 [16], replicated, may hold values from 1540 to 2048
Outputs:
- gram_matrix: float32 [2144, 2144], P('space')
- right_sides: float32 [2144, 64], P('space')
Inputs may be any that keep to these rules, and one draw needn't show every extreme that they name: lengths[k] snapshots of trajectory k are recorded; later positions of its slot of 2048 are padding.
All inputs are finite; a program needn't handle non-finite values.
Results may differ from a plain program's by a relative error of at most 0.0003.
Values sent between devices are 32-bit elements; how exact they have to be, the bound alone decides.
No kernel may reach another device: no remote copies, remote signals or barrier semaphores. Data moves between devices by JAX's collectives and lax.ppermute only.
A program may use at most 64 MiB of HBM per device.

v0:
```python
import jax
import jax.numpy as jnp
import numpy as np
from jax import lax
from jax.sharding import PartitionSpec as P

FEAT = 2144
EXACT = lax.Precision.HIGHEST


def extended(cells, sides, width):
    for axis, dim in sides:
        count = lax.axis_size(axis)
        ends = count - 1
        head = lax.slice_in_dim(cells, 0, width, axis=dim)
        tail = lax.slice_in_dim(cells, cells.shape[dim] - width, cells.shape[dim], axis=dim)
        cells = jnp.concatenate(
            [
                lax.ppermute(tail, axis, [(i, (i + 1) % count) for i in range(ends)]),
                cells,
                lax.ppermute(head, axis, [((i + 1) % count, i) for i in range(ends)]),
            ],
            axis=dim,
        )
    return cells


def selectors(modes_count):
    firsts, seconds = np.triu_indices(modes_count)
    modes = np.arange(modes_count)[:, None]
    pick_first = jnp.asarray((modes == firsts[None, :]).astype(np.float32))
    pick_second = jnp.asarray((modes == seconds[None, :]).astype(np.float32))
    return (pick_first, pick_second)


def features(block_rows):
    pick_first, pick_second = selectors(block_rows.shape[1])
    first = jnp.dot(block_rows, pick_first, precision=EXACT, preferred_element_type=jnp.float32)
    second = jnp.dot(block_rows, pick_second, precision=EXACT, preferred_element_type=jnp.float32)
    return jnp.concatenate([block_rows, first * second], axis=1)


def outer_rows(left_part, right_part):
    return jnp.einsum(
        "tf,tg->fg", left_part, right_part, precision=EXACT, preferred_element_type=jnp.float32
    )


def energy_sum(energy_part):
    return lax.psum(energy_part, ("space", "tm"))


def stencil(padded, width):
    return (
        padded[:, :width]
        - 8.0 * padded[:, 1 : width + 1]
        + 8.0 * padded[:, 3 : width + 3]
        - padded[:, 4:]
    ) / 12.0


def shards(snapshots, basis, lengths):
    partial_value = jnp.einsum("cr,ct->rt", basis, snapshots, preferred_element_type=jnp.float32)
    horizon = partial_value.shape[1]
    time_index = lax.axis_index("tm")
    cell_index = lax.axis_index("space")
    padded = extended(partial_value, (("tm", 1),), 2)
    change_part = stencil(padded, horizon)
    states, change = (
        lax.psum_scatter(partial_value, "space", scatter_dimension=1, tiled=True),
        lax.psum_scatter(change_part, "space", scatter_dimension=1, tiled=True),
    )
    share = states.shape[1]
    slot_width = 2 * horizon
    traj_count = lengths.shape[0]
    shifted = (
        time_index * horizon
        + cell_index * share
        + jnp.arange(share, dtype=jnp.int32)
        + horizon // 2
    )
    offsets = shifted % slot_width
    owners = shifted // slot_width % traj_count
    match = owners[:, None] == jnp.arange(traj_count, dtype=jnp.int32)[None, :]
    limits = jnp.sum(jnp.where(match, lengths[None, :], 0), axis=1)
    living = ((offsets >= 2) & (offsets <= limits - 3)).astype(jnp.float32)
    samples = jnp.sum(lengths - 4).astype(jnp.float32)
    masked = states * living[None, :]
    dmasked = change * living[None, :]
    energy_part = jnp.sum(masked * masked, axis=1)
    row_count = FEAT // lax.axis_size("space")
    scales = jnp.sqrt(energy_sum(energy_part) / samples + 1e-06)
    masked = masked / scales[:, None]
    dmasked = dmasked / scales[:, None]
    whole_states, whole_change = (
        lax.all_gather(masked, "space", axis=1, tiled=True),
        lax.all_gather(dmasked, "space", axis=1, tiled=True),
    )
    design = features(whole_states.T)
    picked = lax.dynamic_slice_in_dim(design, cell_index * row_count, row_count, 1)
    gram_part = outer_rows(picked, design)
    side_part = outer_rows(picked, whole_change.T)
    gram_part, side_part = lax.psum((gram_part, side_part), "tm")
    return (gram_part / samples, side_part / samples)


def solution(mesh):
    return jax.shard_map(
        shards,
        mesh=mesh,
        in_specs=(P("space", "tm"), P("space", None), P()),
        out_specs=(P("space", None), P("space", None)),
        check_vma=False,
    )
```

profile of v0, /device:TPU:8, one launch (start us, length us, event | category | flops | bytes accessed | tf_op | source)
XLA Modules:
  0.0 340.6 jit_solution(10435550340036665465)
XLA Ops:
  7.2 0.0 copy-start
  7.2 0.0 copy-start.2
  7.2 0.0 copy-start.4
  7.2 0.0 reduce-scatter.3.cloned.1.call-start
  7.2 1.5 copy-done
  8.8 2.1 fusion.14
  10.9 0.0 reduce-scatter.3.cloned.1.call-update
  10.9 0.0 reduce-scatter.5.cloned.1.call-start
  10.9 0.9 fusion.13
  11.8 3.8 %collective-permute-start = (f32[64,2]{1,0:T(8,128)S(1)}, f32[64,2]{1,0:T(8,128)S(1)}, u32[]{:S(2)}, u32[]{:S(2)}) collective-permute-start(f32[64,2]{1,0:T(8,128)S(1)} %get-tuple-element.4), channel_id=1, source_target_pairs={{0,1},{1,2},{2,3},{3,4},{4,5},{5,6},{6,7},{7,8},{8,9},{9,10},{10,1... | collective-permute-start | bytes 1544 | tf_op jit(solution)/shard_map/ppermute | solution.py:19
  15.6 1.3 collective-permute-start.1
  16.9 0.0 copy-done.4
  17.0 0.1 select_reduce_fusion
  17.0 0.6 add_reduce_fusion
  18.3 0.0 collective-permute-done
  18.3 3.1 collective-permute-done.1
  21.4 2.4 fusion.7
  23.8 0.0 reduce-scatter.5.cloned.1.call-update
  23.8 0.0 all-reduce.3.cloned.1.call-start
  23.9 20.7 %reduce-scatter.3.cloned.1.call-done = f32[64,128]{1,0:T(8,128)} async-done(((f32[64,1024]{1,0:T(8,128)}), f32[64,128]{1,0:T(8,128)}) %reduce-scatter.3.cloned.1.call-update) | async-done | bytes 32784 | tf_op jit(solution)/shard_map/reduce_scatter | solution.py:70
  44.5 0.9 multiply_reduce_fusion
  45.4 77.0 %psum.21 = f32[64]{0:T(128)S(1)} all-reduce(f32[64]{0:T(128)S(1)} %multiply_reduce_fusion), channel_id=1, replica_groups=mesh['space'=8,'tm'=32] {'space','tm'}, use_global_device_ids=true, to_apply=%region_3.4 | all-reduce | flops 64 | bytes 512 | tf_op jit(solution)/shard_map/psum | solution.py:50
  122.4 0.0 reduce-scatter.5.cloned.1.call-done
  122.4 0.9 multiply_divide_fusion
  123.3 12.9 %all_gather.6 = f32[64,1024]{1,0:T(8,128)S(1)} all-gather(f32[64,128]{1,0:T(8,128)S(1)} %get-tuple-element.7), channel_id=1, replica_groups=mesh['space'=8,'tm'=32] {'space'}, dimensions={1}, use_global_device_ids=true | all-gather | bytes 294912 | tf_op jit(solution)/shard_map/all_gather | solution.py:96
  136.2 0.0 copy-done.2
  136.2 0.0 copy-start.1
  136.2 7.0 %fusion.15 = f32[1024,2080]{0,1:T(8,128)S(1)} fusion(f32[64,1024]{1,0:T(8,128)S(1)} %all_gather.6, f32[64,2080]{1,0:T(8,128)S(1)} %copy-done.2), kind=kOutput, calls=%fused_computation.44 | convolution fusion | flops 1635778560 | bytes 9314304 | tf_op jit(solution)/shard_map/dot_general | solution.py:38
  143.1 0.0 copy-done.1
  143.2 7.3 %convolution_multiply_fusion = f32[1024,2080]{0,1:T(8,128)S(1)} fusion(f32[1024,2080]{0,1:T(8,128)S(1)} %fusion.15, f32[64,1024]{1,0:T(8,128)S(1)} %all_gather.6, f32[64,2080]{1,0:T(8,128)S(1)} %copy-done.1), kind=kOutput, calls=%fused_computation.5 | convolution fusion | flops 1637908480 | bytes 17833984 | tf_op jit(solution)/shard_map/dot_general | solution.py:39
  150.5 0.2 fusion.2
  150.7 9.9 %fusion = f32[268,2144]{1,0:T(8,128)} fusion(f32[1024,268]{0,1:T(8,128)S(1)} %fusion.2, f32[1024,64]{0,1:T(8,128)S(1)} %bitcast.11, f32[1024,2080]{0,1:T(8,128)S(1)} %convolution_multiply_fusion), kind=kOutput, calls=%fused_computation.2 | convolution fusion | flops 7062781952 | bytes 12177920 | tf_op jit(solution)/shard_map/tf,tg->fg/dot_general | solution.py:44
  160.6 12.9 %all_gather.7 = f32[64,1024]{1,0:T(8,128)S(1)} all-gather(f32[64,128]{1,0:T(8,128)S(1)} %get-tuple-element.6), channel_id=1, replica_groups=mesh['space'=8,'tm'=32] {'space'}, dimensions={1}, use_global_device_ids=true | all-gather | bytes 294912 | tf_op jit(solution)/shard_map/all_gather | solution.py:97
  173.5 1.9 fusion.16
  175.4 0.0 all-reduce.3.cloned.1.call-update
  175.4 154.8 %all-reduce.3.cloned.1.call-done = (f32[268,2144]{1,0:T(8,128)}, f32[268,64]{0,1:T(8,128)}) async-done(((f32[268,2144]{1,0:T(8,128)}, f32[268,64]{0,1:T(8,128)}), (f32[268,2144]{1,0:T(8,128)}, f32[268,64]{0,1:T(8,128)})) %all-reduce.3.cloned.1.call-update) | async-done | bytes 2366992 | tf_op jit(solution)/shard_map/psum | solution.py:103
  330.2 0.0 copy-start.3
  330.2 3.3 broadcast_divide_fusion
  333.5 0.0 copy-done.3
  333.5 0.7 broadcast_divide_fusion.1
  (3 shorter events, 0.0 us)
Async XLA Ops:
  7.2 1.6 copy-start
  7.2 129.0 %copy-start.2 = (f32[64,2080]{1,0:T(8,128)S(1)}, f32[64,2080]{1,0:T(8,128)}, u32[]{:S(2)}) copy-start(f32[64,2080]{1,0:T(8,128)} %constant.80.clone) | copy-start | bytes 1597444
  7.2 9.8 %copy-start.4 = (s32[16]{0:T(128)S(1)}, s32[16]{0:T(128)}, u32[]{:S(2)}) copy-start(s32[16]{0:T(128)} %param.7) | copy-start | bytes 196
  7.2 37.3 %reduce-scatter.3.cloned.1.call-start = ((), (), s32[]{:S(2)}) async-start(), calls=%async_computation.2 | async-start | bytes 294912 | tf_op jit(solution)/shard_map/reduce_scatter | solution.py:70
  10.9 111.5 %reduce-scatter.5.cloned.1.call-start = ((), (), s32[]{:S(2)}) async-start(), calls=%async_computation.3 | async-start | bytes 294912 | tf_op jit(solution)/shard_map/reduce_scatter | solution.py:71
  11.8 6.5 %collective-permute-start = (f32[64,2]{1,0:T(8,128)S(1)}, f32[64,2]{1,0:T(8,128)S(1)}, u32[]{:S(2)}, u32[]{:S(2)}) collective-permute-start(f32[64,2]{1,0:T(8,128)S(1)} %get-tuple-element.4), channel_id=1, source_target_pairs={{0,1},{1,2},{2,3},{3,4},{4,5},{5,6},{6,7},{7,8},{8,9},{9,10},{10,1... | collective-permute-start | bytes 1544 | tf_op jit(solution)/shard_map/ppermute | solution.py:19
  15.6 5.8 %collective-permute-start.1 = (f32[64,2]{1,0:T(8,128)S(1)}, f32[64,2]{1,0:T(8,128)S(1)}, u32[]{:S(2)}, u32[]{:S(2)}) collective-permute-start(f32[64,2]{1,0:T(8,128)S(1)} %get-tuple-element.5), channel_id=1, source_target_pairs={{1,0},{2,1},{3,2},{4,3},{5,4},{6,5},{7,6},{8,7},{9,8},{10,9},{11,1... | collective-permute-start | bytes 1544 | tf_op jit(solution)/shard_map/ppermute | solution.py:21
  23.8 306.4 %all-reduce.3.cloned.1.call-start = ((), (), s32[]{:S(2)}) async-start(), calls=%async_computation.4 | async-start | bytes 4931584 | tf_op jit(solution)/shard_map/psum | solution.py:103
  136.2 7.0 %copy-start.1 = (f32[64,2080]{1,0:T(8,128)S(1)}, f32[64,2080]{1,0:T(8,128)}, u32[]{:S(2)}) copy-start(f32[64,2080]{1,0:T(8,128)} %constant.81.clone) | copy-start | bytes 1597444
  330.2 3.3 copy-start.3
Sparse Core Ops, SparseCore 0:
  11.1 33.4 reduce-scatter.2
  47.0 32.4 reduce-scatter.4
  175.6 154.5 all-reduce.2
where the time goes:
time: 341 us
  waiting for transfers between devices  179 us (52%)
  blocking collectives  103 us (30%)
  matrix products  28.1 us (8%)
  between operations  14.5 us (4%)
  other arithmetic  8.98 us (3%)
  starting transfers between devices  5.23 us (2%)
    psum x1, waiting for transfers between devices, shards(): gram_part, side_part = lax.psum((gram_part, side_part), 'tm')  155 us
    psum x1, blocking collectives, energy_sum(): return lax.psum(energy_part, ('space', 'tm'))  77 us
    reduce_scatter x1, waiting for transfers between devices, shards(): lax.psum_scatter(partial_value, 'space', scatter_dimension=1, tiled=True)  20.7 us
    all_gather x1, blocking collectives, shards(): lax.all_gather(dmasked, 'space', axis=1, tiled=True)  12.9 us
    all_gather x1, blocking collectives, shards(): lax.all_gather(masked, 'space', axis=1, tiled=True)  12.9 us
    dot_general x2, matrix products, outer_rows(): jnp.einsum('tf,tg->fg', left_part, right_part, precision=EXACT, preferred...  11.8 us
    dot_general x1, matrix products, features(): jnp.dot(block_rows, pick_second, precision=EXACT, preferred_element_type=...  7.29 us
    dot_general x1, matrix products, features(): jnp.dot(block_rows, pick_first, precision=EXACT, preferred_element_type=j...  6.96 us
  transfers between devices with their start and end apart: 5, of which 3 were waited for; matrix products, arithmetic and copies ran while one was open for 1% of the time, Pallas kernels for 0%

commit v1 on v0

--- a/solution.py
+++ b/solution.py
@@ -47,7 +47,7 @@
 
 
 def energy_sum(energy_part):
-    return lax.psum(energy_part, ("space", "tm"))
+    return jnp.sum(lax.all_gather(energy_part, ("space", "tm")), axis=0)
 
 
 def stencil(padded, width):

time: 341 us -> 546 us (1.60)
  waiting for transfers between devices: 179 us -> 458 us
  blocking collectives: 103 us -> 26.3 us
    unnamed x3 -> x5, waiting for transfers between devices: 0.05 us -> 243 us
    psum x1 -> x0, blocking collectives: 77 us -> none  [energy_sum(): return lax.psum(energy_part, ('space', 'tm'))]
    reduce_scatter x1, waiting for transfers between devices: 0.01 us -> 29.4 us  [shards(): lax.psum_scatter(change_part, 'space', scatter_dimension=1, tiled=True)]
    reduce_scatter x1, waiting for transfers between devices: 20.7 us -> 27.5 us  [shards(): lax.psum_scatter(partial_value, 'space', scatter_dimension=1, tiled=True)]
  transfers between devices with their start and end apart: 5 -> 6, of which waited for: 3 -> 4; matrix products, arithmetic and copies ran while one was open for 1% -> 1% of each run, Pallas kernels for 0% -> 0%
where the time goes in v1:
time: 546 us; the launch traced here: 545 us
  waiting for transfers between devices  458 us (84%)
  matrix products  28.1 us (5%)
  blocking collectives  26.3 us (5%)
  between operations  14.6 us (3%)
  other arithmetic  9.04 us (2%)
    unnamed x5, waiting for transfers between devices  243 us
    psum x1, waiting for transfers between devices, shards(): gram_part, side_part = lax.psum((gram_part, side_part), 'tm')  158 us
    reduce_scatter x1, waiting for transfers between devices, shards(): lax.psum_scatter(change_part, 'space', scatter_dimension=1, tiled=True)  29.4 us
    reduce_scatter x1, waiting for transfers between devices, shards(): lax.psum_scatter(partial_value, 'space', scatter_dimension=1, tiled=True)  27.5 us
    all_gather x1, blocking collectives, shards(): lax.all_gather(masked, 'space', axis=1, tiled=True)  13.3 us
    all_gather x1, blocking collectives, shards(): lax.all_gather(dmasked, 'space', axis=1, tiled=True)  13 us
    dot_general x2, matrix products, outer_rows(): jnp.einsum('tf,tg->fg', left_part, right_part, precision=EXACT, preferred...  11.8 us
  transfers between devices with their start and end apart: 6, of which 4 were waited for; matrix products, arithmetic and copies ran while one was open for 1% of the time, Pallas kernels for 0%

profile of v1, /device:TPU:8, one launch (start us, length us, event | category | flops | bytes accessed | tf_op | source)
XLA Modules:
  0.0 545.3 jit_solution(5896335886816280176)
XLA Ops:
  7.2 0.0 copy-start
  7.2 0.0 copy-start.2
  7.2 0.0 copy-start.5
  7.2 0.0 reduce-scatter.3.cloned.1.call-start
  7.2 1.5 copy-done
  8.8 2.1 fusion.14
  10.9 0.0 reduce-scatter.3.cloned.1.call-update
  10.9 0.0 all-reduce.5.cloned.1.call-start
  10.9 0.9 fusion.13
  11.8 3.8 collective-permute-start
  15.6 1.3 collective-permute-start.1
  16.9 0.0 copy-done.5
  17.0 0.1 select_reduce_fusion
  17.1 27.5 %reduce-scatter.3.cloned.1.call-done = f32[64,128]{1,0:T(8,128)} async-done(((f32[64,1024]{1,0:T(8,128)}), f32[64,128]{1,0:T(8,128)}) %reduce-scatter.3.cloned.1.call-update) | async-done | bytes 32784 | tf_op jit(solution)/shard_map/reduce_scatter | solution.py:70
  44.5 0.9 multiply_reduce_fusion
  45.4 0.3 dynamic-update-slice
  45.7 0.0 copy-start.3
  45.7 0.6 copy-done.3
  46.3 0.0 all-reduce.5.cloned.1.call-update
  46.4 0.0 reduce-scatter.5.cloned.1.call-start
  46.4 0.0 collective-permute-done
  46.4 0.0 collective-permute-done.1
  46.4 2.4 fusion.7
  48.8 0.0 reduce-scatter.5.cloned.1.call-update
  48.8 0.0 all-reduce.7.cloned.1.call-start
  48.9 0.6 add_reduce_fusion
  50.2 242.9 %all-reduce.5.cloned.1.call-done = f32[16384]{0:T(1024)} async-done(((f32[16384]{0:T(1024)}), f32[16384]{0:T(1024)}) %all-reduce.5.cloned.1.call-update) | async-done | bytes 65552
  293.1 0.9 reshape.64
  294.0 0.1 reduce_sum.38
  294.1 29.4 %reduce-scatter.5.cloned.1.call-done = f32[64,128]{1,0:T(8,128)} async-done(((f32[64,1024]{1,0:T(8,128)}), f32[64,128]{1,0:T(8,128)}) %reduce-scatter.5.cloned.1.call-update) | async-done | bytes 32784 | tf_op jit(solution)/shard_map/reduce_scatter | solution.py:71
  323.5 0.9 multiply_divide_fusion
  324.3 13.3 %all_gather.14 = f32[64,1024]{1,0:T(8,128)S(1)} all-gather(f32[64,128]{1,0:T(8,128)S(1)} %get-tuple-element.7), channel_id=1, replica_groups=mesh['space'=8,'tm'=32] {'space'}, dimensions={1}, use_global_device_ids=true | all-gather | bytes 294912 | tf_op jit(solution)/shard_map/all_gather | solution.py:96
  337.6 0.0 copy-done.2
  337.6 0.0 copy-start.1
  337.6 7.0 %fusion.15 = f32[1024,2080]{0,1:T(8,128)S(1)} fusion(f32[64,1024]{1,0:T(8,128)S(1)} %all_gather.14, f32[64,2080]{1,0:T(8,128)S(1)} %copy-done.2), kind=kOutput, calls=%fused_computation.44 | convolution fusion | flops 1635778560 | bytes 9314304 | tf_op jit(solution)/shard_map/dot_general | solution.py:38
  344.6 0.0 copy-done.1
  344.6 7.3 %convolution_multiply_fusion = f32[1024,2080]{0,1:T(8,128)S(1)} fusion(f32[1024,2080]{0,1:T(8,128)S(1)} %fusion.15, f32[64,1024]{1,0:T(8,128)S(1)} %all_gather.14, f32[64,2080]{1,0:T(8,128)S(1)} %copy-done.1), kind=kOutput, calls=%fused_computation.5 | convolution fusion | flops 1637908480 | bytes 17833984 | tf_op jit(solution)/shard_map/dot_general | solution.py:39
  351.9 0.2 fusion.2
  352.1 9.9 %fusion = f32[268,2144]{1,0:T(8,128)} fusion(f32[1024,268]{0,1:T(8,128)S(1)} %fusion.2, f32[1024,64]{0,1:T(8,128)S(1)} %bitcast.11, f32[1024,2080]{0,1:T(8,128)S(1)} %convolution_multiply_fusion), kind=kOutput, calls=%fused_computation.2 | convolution fusion | flops 7062781952 | bytes 12177920 | tf_op jit(solution)/shard_map/tf,tg->fg/dot_general | solution.py:44
  362.0 13.0 %all_gather.15 = f32[64,1024]{1,0:T(8,128)S(1)} all-gather(f32[64,128]{1,0:T(8,128)S(1)} %get-tuple-element.6), channel_id=1, replica_groups=mesh['space'=8,'tm'=32] {'space'}, dimensions={1}, use_global_device_ids=true | all-gather | bytes 294912 | tf_op jit(solution)/shard_map/all_gather | solution.py:97
  375.0 1.9 fusion.16
  376.9 0.0 all-reduce.7.cloned.1.call-update
  376.9 157.9 %all-reduce.7.cloned.1.call-done = (f32[268,2144]{1,0:T(8,128)}, f32[268,64]{0,1:T(8,128)}) async-done(((f32[268,2144]{1,0:T(8,128)}, f32[268,64]{0,1:T(8,128)}), (f32[268,2144]{1,0:T(8,128)}, f32[268,64]{0,1:T(8,128)})) %all-reduce.7.cloned.1.call-update) | async-done | bytes 2366992 | tf_op jit(solution)/shard_map/psum | solution.py:103
  534.9 0.0 copy-start.4
  534.9 3.3 broadcast_divide_fusion
  538.1 0.0 copy-done.4
  538.1 0.7 broadcast_divide_fusion.1
  (4 shorter events, 0.1 us)
Async XLA Ops:
  7.2 1.6 copy-start
  7.2 330.4 %copy-start.2 = (f32[64,2080]{1,0:T(8,128)S(1)}, f32[64,2080]{1,0:T(8,128)}, u32[]{:S(2)}) copy-start(f32[64,2080]{1,0:T(8,128)} %constant.80.clone) | copy-start | bytes 1597444
  7.2 9.8 %copy-start.5 = (s32[16]{0:T(128)S(1)}, s32[16]{0:T(128)}, u32[]{:S(2)}) copy-start(s32[16]{0:T(128)} %param.7) | copy-start | bytes 196
  7.2 37.3 %reduce-scatter.3.cloned.1.call-start = ((), (), s32[]{:S(2)}) async-start(), calls=%async_computation.2 | async-start | bytes 294912 | tf_op jit(solution)/shard_map/reduce_scatter | solution.py:70
  10.9 282.2 %all-reduce.5.cloned.1.call-start = ((), (), s32[]{:S(2)}) async-start(), calls=%async_computation.4 | async-start | bytes 131072
  11.8 34.6 %collective-permute-start = (f32[64,2]{1,0:T(8,128)S(1)}, f32[64,2]{1,0:T(8,128)S(1)}, u32[]{:S(2)}, u32[]{:S(2)}) collective-permute-start(f32[64,2]{1,0:T(8,128)S(1)} %get-tuple-element.4), channel_id=1, source_target_pairs={{0,1},{1,2},{2,3},{3,4},{4,5},{5,6},{6,7},{7,8},{8,9},{9,10},{10,1... | collective-permute-start | bytes 1544 | tf_op jit(solution)/shard_map/ppermute | solution.py:19
  15.6 30.8 %collective-permute-start.1 = (f32[64,2]{1,0:T(8,128)S(1)}, f32[64,2]{1,0:T(8,128)S(1)}, u32[]{:S(2)}, u32[]{:S(2)}) collective-permute-start(f32[64,2]{1,0:T(8,128)S(1)} %get-tuple-element.5), channel_id=1, source_target_pairs={{1,0},{2,1},{3,2},{4,3},{5,4},{6,5},{7,6},{8,7},{9,8},{10,9},{11,1... | collective-permute-start | bytes 1544 | tf_op jit(solution)/shard_map/ppermute | solution.py:21
  45.7 0.6 copy-start.3
  46.4 277.1 %reduce-scatter.5.cloned.1.call-start = ((), (), s32[]{:S(2)}) async-start(), calls=%async_computation.3 | async-start | bytes 294912 | tf_op jit(solution)/shard_map/reduce_scatter | solution.py:71
  48.8 486.0 %all-reduce.7.cloned.1.call-start = ((), (), s32[]{:S(2)}) async-start(), calls=%async_computation.5 | async-start | bytes 4931584 | tf_op jit(solution)/shard_map/psum | solution.py:103
  337.6 7.0 %copy-start.1 = (f32[64,2080]{1,0:T(8,128)S(1)}, f32[64,2080]{1,0:T(8,128)}, u32[]{:S(2)}) copy-start(f32[64,2080]{1,0:T(8,128)} %constant.81.clone) | copy-start | bytes 1597444
  534.9 3.3 copy-start.4
Sparse Core Ops, SparseCore 0:
  11.1 33.4 reduce-scatter.2
  50.6 242.3 all-reduce.4
  295.6 27.8 reduce-scatter.4
  377.1 157.7 all-reduce.6
